TPU v7x, 32 devices: a whole 2x2x4 slice. The times are simulated.
32 devices in a mesh: fsdp: 4 (over y, x), heads: 2 (over core), tensor: 4 (over z).
Axes of the slice: x: 2, y: 2, z: 4, core: 2. Of those that a mesh axis runs over, the one named last changes fastest.
Arguments:
- inputs: float32 [32, 729, 1152], P(('fsdp', 'heads', 'tensor')), may hold values from -6 to 6
- cotangent: float32 [32, 729, 1152], P(('fsdp', 'heads', 'tensor')), may hold values from -6 to 6
- image_adapter_index: int32 [32], replicated, may hold values from 0 to 7
- first_norm_gain: float32 [1152], replicated, may hold values from 0.5 to 1.5
- first_norm_bias: float32 [1152], replicated, may hold values from -3 to 3
- second_norm_gain: float32 [1152], replicated, may hold values from 0.5 to 1.5
- second_norm_bias: float32 [1152], replicated, may hold values from -3 to 3
- query_key_value_weight: bfloat16 [1152, 3, 1152], P('fsdp', None, 'heads'), may hold values from -0.1875 to 0.1875
- attention_output_weight: bfloat16 [1152, 1152], P('fsdp', 'heads'), may hold values from -3 to 3
- up_weight: bfloat16 [1152, 4304], P('fsdp', 'tensor'), may hold values from -0.1875 to 0.1875
- down_weight: bfloat16 [1152, 4304], P('fsdp', 'tensor'), may hold values from -0.09375 to 0.09375
- up_projection_bias: bfloat16 [4304], P('tensor'), may hold values from -3 to 3
- down_projection_bias: bfloat16 [1152], replicated, may hold values from -3 to 3
- query_key_value_adapter_first: bfloat16 [3, 8, 1152, 16], replicated, may hold values from -0.1875 to 0.1875
- query_key_value_adapter_second: bfloat16 [3, 8, 16, 1152], P(None, None, None, 'heads'), may hold values from -0.75 to 0.75
- projection_adapter_first: bfloat16 [8, 1152, 16], P(None, 'heads'), may hold values from -3 to 3
- projection_adapter_second: bfloat16 [8, 16, 1152], replicated, may hold values from -0.75 to 0.75
- up_adapter_first: bfloat16 [8, 1152, 16], replicated, may hold values from -0.1875 to 0.1875
- up_adapter_second: bfloat16 [8, 16, 4304], P(None, None, 'tensor'), may hold values from -0.75 to 0.75
- down_adapter_first: bfloat16 [8, 16, 4304], P(None, None, 'tensor'), may hold values from -0.09375 to 0.09375
- down_adapter_second: bfloat16 [8, 16, 1152], replicated, may hold values from -0.75 to 0.75
Outputs:
- layer_output: float32 [32, 729, 1152], P(('fsdp', 'heads', 'tensor'))
- grad_input: float32 [32, 729, 1152], P(('fsdp', 'heads', 'tensor'))
- grad_qkv_in: float32 [3, 8, 1152, 16], replicated
- grad_qkv_out: float32 [3, 8, 16, 1152], P(None, None, None, 'heads')
- grad_proj_in: float32 [8, 1152, 16], P(None, 'heads')
- grad_proj_out: float32 [8, 16, 1152], replicated
- grad_up_in: float32 [8, 1152, 16], replicated
- grad_up_out: float32 [8, 16, 4304], P(None, None, 'tensor')
- grad_down_in: float32 [8, 16, 4304], P(None, None, 'tensor')
- grad_down_out: float32 [8, 16, 1152], replicated
All inputs are finite; a program needn't handle non-finite values.
Results may differ from a plain program's by a relative error of at most 0.02.
Values may be sent and summed in bfloat16 or wider, within the bound.
A program may use at most 256 MiB of HBM per device.

v0:
```python
import jax
import jax.numpy as jnp
from jax import lax
from jax.sharding import PartitionSpec as P

HEAD_DIM = 72
highest_precision = lax.Precision.HIGHEST
norm_eps = 1e-06


def normalize(values, gain, bias):
    mean = jnp.mean(values, axis=-1, keepdims=True)
    centred = values - mean
    inverse = lax.rsqrt(jnp.mean(centred * centred, axis=-1, keepdims=True) + norm_eps)
    unit = centred * inverse
    return (unit * gain + bias, unit, inverse)


def normalize_back(grad_norm, unit, inverse, gain):
    scaled = grad_norm * gain
    return inverse * (
        scaled
        - jnp.mean(scaled, axis=-1, keepdims=True)
        - unit * jnp.mean(scaled * unit, axis=-1, keepdims=True)
    )


def gelu_tanh(values):
    return jax.nn.gelu(values, approximate=True)


def one_hot(ids, count):
    return (ids[:, None] == jnp.arange(count, dtype=jnp.int32)[None, :]).astype(jnp.float32)


def by_adapter(hot, per_image):
    return jnp.einsum("ia,ixy->axy", hot, per_image, precision=highest_precision)


def attend_forward(operands):
    query, keyed, valued = operands
    scores = jnp.einsum(
        "qhd,khd->hqk", query, keyed, preferred_element_type=jnp.float32
    ) * HEAD_DIM ** (-0.5)
    top = jnp.max(scores, axis=-1, keepdims=True)
    weights = jnp.exp(scores - top)
    total = jnp.sum(weights, axis=-1, keepdims=True)
    probs = (weights / total).astype(jnp.bfloat16)
    mixed_heads = jnp.einsum("hqk,khd->qhd", probs, valued, preferred_element_type=jnp.float32)
    return (mixed_heads.astype(jnp.bfloat16), (top + jnp.log(total))[..., 0])


def attend_back(operands):
    query, keyed, valued, grad_mixed, log_total = operands
    scale = HEAD_DIM ** (-0.5)
    scores = jnp.einsum("qhd,khd->hqk", query, keyed, preferred_element_type=jnp.float32) * scale
    probs = jnp.exp(scores - log_total[..., None])
    grad_probs = jnp.einsum("qhd,khd->hqk", grad_mixed, valued, preferred_element_type=jnp.float32)
    grad_values = jnp.einsum(
        "hqk,qhd->khd", probs.astype(jnp.bfloat16), grad_mixed, preferred_element_type=jnp.float32
    )
    inner = jnp.sum(probs * grad_probs, axis=-1, keepdims=True)
    grad_scores = (probs * (grad_probs - inner)).astype(jnp.bfloat16)
    grad_query = (
        jnp.einsum("hqk,khd->qhd", grad_scores, keyed, preferred_element_type=jnp.float32) * scale
    )
    grad_keys = (
        jnp.einsum("hqk,qhd->khd", grad_scores, query, preferred_element_type=jnp.float32) * scale
    )
    return (grad_query, grad_keys, grad_values)


def per_device(
    inputs,
    cotangent,
    image_adapter_index,
    first_norm_gain,
    first_norm_bias,
    second_norm_gain,
    second_norm_bias,
    query_key_value_weight,
    attention_output_weight,
    up_weight,
    down_weight,
    up_projection_bias,
    down_projection_bias,
    query_key_value_adapter_first,
    query_key_value_adapter_second,
    projection_adapter_first,
    projection_adapter_second,
    up_adapter_first,
    up_adapter_second,
    down_adapter_first,
    down_adapter_second,
):
    head_count = lax.axis_size("heads")
    unit_count = lax.axis_size("tensor")
    fsdp_index = lax.axis_index("fsdp")
    head_index = lax.axis_index("heads")
    unit_index = lax.axis_index("tensor")
    images, length, width = inputs.shape
    adapter_factors = query_key_value_adapter_first.shape[1]
    local = jnp.arange(images, dtype=jnp.int32)
    group = fsdp_index * head_count
    own_rows = ((group + head_index) * unit_count + unit_index) * images + local
    head_rows = (
        ((group + jnp.arange(head_count, dtype=jnp.int32))[:, None] * unit_count + unit_index)
        * images
        + local[None, :]
    ).reshape(-1)
    unit_rows = (
        ((group + head_index) * unit_count + jnp.arange(unit_count, dtype=jnp.int32))[:, None]
        * images
        + local[None, :]
    ).reshape(-1)
    owned_numbers = image_adapter_index[own_rows]
    head_numbers = image_adapter_index[head_rows]
    unit_numbers = image_adapter_index[unit_rows]
    query_key_value_whole, output_whole_weight, up_rows, down_rows = (
        lax.all_gather(query_key_value_weight, "fsdp", axis=0, tiled=True),
        lax.all_gather(attention_output_weight, "fsdp", axis=0, tiled=True),
        lax.all_gather(up_weight, "fsdp", axis=0, tiled=True),
        lax.all_gather(down_weight, "fsdp", axis=0, tiled=True),
    )
    norm1, unit1, inverse1 = normalize(inputs, first_norm_gain, first_norm_bias)
    ln1_all = lax.all_gather(norm1.astype(jnp.bfloat16), "heads", axis=0, tiled=True)
    (
        query_key_value_attention,
        output_attention_part,
        query_key_value_output_weight,
        projection_input_weight,
    ) = (
        query_key_value_whole,
        output_whole_weight,
        query_key_value_adapter_second,
        projection_adapter_first,
    )
    seen = ln1_all.shape[0]
    query_key_value_input_selected = query_key_value_adapter_first[:, head_numbers]
    qkv_out_sel = query_key_value_output_weight[:, head_numbers]
    query_key_value_middle = jnp.einsum(
        "obl,holm->hobm",
        ln1_all,
        query_key_value_input_selected,
        preferred_element_type=jnp.float32,
    )
    projected = jnp.einsum(
        "isd,djf->jisf", ln1_all, query_key_value_attention, preferred_element_type=jnp.float32
    )
    projected = projected + jnp.einsum(
        "klty,klye->klte",
        query_key_value_middle,
        qkv_out_sel.astype(jnp.float32),
        precision=highest_precision,
    )
    proj_low = projected.astype(jnp.bfloat16)
    local_width = proj_low.shape[-1]
    heads_local = local_width // HEAD_DIM
    shaped = proj_low.reshape(3, seen, length, heads_local, HEAD_DIM)
    mixed_heads, log_total = lax.map(attend_forward, (shaped[0], shaped[1], shaped[2]))
    mixed_heads = mixed_heads.reshape(seen, length, local_width)
    proj_in_sel = projection_input_weight[head_numbers]
    projection_output_selected = projection_adapter_second[head_numbers]
    projection_adapter_middle = jnp.einsum(
        "lby,lyg->lbg", mixed_heads, proj_in_sel, preferred_element_type=jnp.float32
    )
    attention_branch = jnp.einsum(
        "ise,de->isd", mixed_heads, output_attention_part, preferred_element_type=jnp.float32
    )
    attention_branch = attention_branch + jnp.einsum(
        "cmt,ctf->cmf",
        projection_adapter_middle,
        projection_output_selected.astype(jnp.float32),
        precision=highest_precision,
    )
    hidden = inputs + lax.psum_scatter(
        attention_branch.astype(jnp.bfloat16), "heads", scatter_dimension=0, tiled=True
    ).astype(jnp.float32)
    norm2, unit2, inverse2 = normalize(hidden, second_norm_gain, second_norm_bias)
    second_norm_reduced = norm2.astype(jnp.bfloat16)
    up_adapter_middle = jnp.einsum(
        "ego,eoh->egh",
        second_norm_reduced,
        up_adapter_first[owned_numbers],
        preferred_element_type=jnp.float32,
    ).astype(jnp.bfloat16)
    ln2_in, up_mid_in = (
        lax.all_gather(second_norm_reduced, "tensor", axis=0, tiled=True),
        lax.all_gather(up_adapter_middle, "tensor", axis=0, tiled=True),
    )
    up_cols, down_cols, bias_cols = (up_rows, down_rows, up_projection_bias)
    up_output_columns, down_input_columns = (up_adapter_second, down_adapter_first)
    up_input_selected = up_adapter_first[unit_numbers]
    up_out_sel = up_output_columns[unit_numbers]
    down_in_sel = down_input_columns[unit_numbers]
    down_output_selected = down_adapter_second[unit_numbers]
    residual_before = jnp.einsum(
        "isd,df->isf", ln2_in, up_cols, preferred_element_type=jnp.float32
    ) + bias_cols.astype(jnp.float32)
    residual_before = residual_before + jnp.einsum(
        "cbd,cdp->cbp",
        up_mid_in.astype(jnp.float32),
        up_out_sel.astype(jnp.float32),
        precision=highest_precision,
    )
    act_low = gelu_tanh(residual_before).astype(jnp.bfloat16)
    down_adapter_middle = jnp.einsum(
        "pco,pqo->pcq", act_low, down_in_sel, preferred_element_type=jnp.float32
    )
    mlp_part = jnp.einsum("isf,df->isd", act_low, down_cols, preferred_element_type=jnp.float32)
    mlp_part = mlp_part + jnp.einsum(
        "cmt,ctf->cmf",
        down_adapter_middle,
        down_output_selected.astype(jnp.float32),
        precision=highest_precision,
    )
    mlp_sum = lax.psum_scatter(
        mlp_part.astype(jnp.bfloat16), "tensor", scatter_dimension=0, tiled=True
    ).astype(jnp.float32)
    layer_output = hidden + mlp_sum + down_projection_bias.astype(jnp.float32)
    grad_mlp = cotangent.astype(jnp.bfloat16)
    grad_mlp_in = lax.all_gather(grad_mlp, "tensor", axis=0, tiled=True)
    grad_down_mid = jnp.einsum(
        "isd,ird->isr", grad_mlp_in, down_output_selected, preferred_element_type=jnp.float32
    )
    grad_act = jnp.einsum("isd,df->isf", grad_mlp_in, down_cols, preferred_element_type=jnp.float32)
    grad_act = grad_act + jnp.einsum(
        "cbd,cdp->cbp", grad_down_mid, down_in_sel.astype(jnp.float32), precision=highest_precision
    )
    ignored, gelu_pull = jax.vjp(gelu_tanh, residual_before)
    grad_before = gelu_pull(grad_act)[0].astype(jnp.bfloat16)
    grad_up_mid = jnp.einsum(
        "pco,pqo->pcq", grad_before, up_out_sel, preferred_element_type=jnp.float32
    )
    grad_ln2 = jnp.einsum("isf,df->isd", grad_before, up_cols, preferred_element_type=jnp.float32)
    grad_ln2 = grad_ln2 + jnp.einsum(
        "isr,idr->isd",
        grad_up_mid,
        up_input_selected.astype(jnp.float32),
        precision=highest_precision,
    )
    grad_ln2 = lax.psum_scatter(
        grad_ln2.astype(jnp.bfloat16), "tensor", scatter_dimension=0, tiled=True
    ).astype(jnp.float32)
    grad_hidden = cotangent + normalize_back(grad_ln2, unit2, inverse2, second_norm_gain)
    mlp_hot = one_hot(unit_numbers, adapter_factors)
    grad_up_in_part = by_adapter(
        mlp_hot, jnp.einsum("isd,isr->idr", ln2_in, grad_up_mid, precision=highest_precision)
    )
    grad_up_out_part = by_adapter(
        mlp_hot,
        jnp.einsum("isr,isf->irf", up_mid_in, grad_before, preferred_element_type=jnp.float32),
    )
    grad_down_in_part = by_adapter(
        mlp_hot, jnp.einsum("isr,isf->irf", grad_down_mid, act_low, precision=highest_precision)
    )
    grad_down_out_part = by_adapter(
        mlp_hot,
        jnp.einsum("isr,isd->ird", down_adapter_middle, grad_mlp_in, precision=highest_precision),
    )
    grad_branch = lax.all_gather(grad_hidden.astype(jnp.bfloat16), "heads", axis=0, tiled=True)
    grad_proj_mid = jnp.einsum(
        "isd,ird->isr", grad_branch, projection_output_selected, preferred_element_type=jnp.float32
    )
    grad_mixed = jnp.einsum(
        "isd,de->ise", grad_branch, output_attention_part, preferred_element_type=jnp.float32
    )
    grad_mixed = grad_mixed + jnp.einsum(
        "isr,ier->ise", grad_proj_mid, proj_in_sel.astype(jnp.float32), precision=highest_precision
    )
    grad_mixed = grad_mixed.astype(jnp.bfloat16).reshape(seen, length, heads_local, HEAD_DIM)
    grad_query, grad_keys, grad_values = lax.map(
        attend_back, (shaped[0], shaped[1], shaped[2], grad_mixed, log_total)
    )
    grad_proj = (
        jnp.stack([grad_query, grad_keys, grad_values])
        .reshape(3, seen, length, local_width)
        .astype(jnp.bfloat16)
    )
    grad_qkv_mid = jnp.einsum(
        "jisf,jirf->jisr", grad_proj, qkv_out_sel, preferred_element_type=jnp.float32
    )
    grad_ln1 = jnp.einsum(
        "jisf,djf->isd", grad_proj, query_key_value_attention, preferred_element_type=jnp.float32
    )
    grad_ln1 = grad_ln1 + jnp.einsum(
        "jisr,jidr->isd",
        grad_qkv_mid,
        query_key_value_input_selected.astype(jnp.float32),
        precision=highest_precision,
    )
    grad_ln1 = lax.psum_scatter(
        grad_ln1.astype(jnp.bfloat16), "heads", scatter_dimension=0, tiled=True
    ).astype(jnp.float32)
    grad_input = grad_hidden + normalize_back(grad_ln1, unit1, inverse1, first_norm_gain)
    attn_hot = one_hot(head_numbers, adapter_factors)
    qkv_in_image = jnp.einsum("isd,jisr->jidr", ln1_all, grad_qkv_mid, precision=highest_precision)
    grad_qkv_in_part = jnp.einsum(
        "ia,jidr->jadr", attn_hot, qkv_in_image, precision=highest_precision
    )
    qkv_out_image = jnp.einsum(
        "jisr,jisf->jirf", query_key_value_middle, grad_proj, precision=highest_precision
    )
    grad_qkv_out_part = jnp.einsum(
        "ia,jirf->jarf", attn_hot, qkv_out_image, precision=highest_precision
    )
    grad_proj_in_part = by_adapter(
        attn_hot,
        jnp.einsum("ise,isr->ier", mixed_heads, grad_proj_mid, precision=highest_precision),
    )
    grad_proj_out_part = by_adapter(
        attn_hot,
        jnp.einsum(
            "isr,isd->ird", projection_adapter_middle, grad_branch, precision=highest_precision
        ),
    )
    grad_qkv_in, grad_proj_out, grad_up_in, grad_down_out = lax.psum(
        (grad_qkv_in_part, grad_proj_out_part, grad_up_in_part, grad_down_out_part),
        ("fsdp", "heads", "tensor"),
    )
    grad_qkv_out, grad_proj_in = lax.psum(
        (grad_qkv_out_part, grad_proj_in_part), ("fsdp", "tensor")
    )
    grad_up_out, grad_down_in = (
        lax.psum(grad_up_out_part.astype(jnp.bfloat16), ("fsdp", "heads")).astype(jnp.float32),
        lax.psum(grad_down_in_part.astype(jnp.bfloat16), ("fsdp", "heads")).astype(jnp.float32),
    )
    return (
        layer_output,
        grad_input,
        grad_qkv_in,
        grad_qkv_out,
        grad_proj_in,
        grad_proj_out,
        grad_up_in,
        grad_up_out,
        grad_down_in,
        grad_down_out,
    )


def solution(mesh):
    in_specs = (
        P(("fsdp", "heads", "tensor"), None, None),
        P(("fsdp", "heads", "tensor"), None, None),
        P(),
        P(),
        P(),
        P(),
        P(),
        P("fsdp", None, "heads"),
        P("fsdp", "heads"),
        P("fsdp", "tensor"),
        P("fsdp", "tensor"),
        P("tensor"),
        P(),
        P(),
        P(None, None, None, "heads"),
        P(None, "heads", None),
        P(),
        P(),
        P(None, None, "tensor"),
        P(None, None, "tensor"),
        P(),
    )
    out_specs = (
        P(("fsdp", "heads", "tensor"), None, None),
        P(("fsdp", "heads", "tensor"), None, None),
        P(),
        P(None, None, None, "heads"),
        P(None, "heads", None),
        P(),
        P(),
        P(None, None, "tensor"),
        P(None, None, "tensor"),
        P(),
    )
    return jax.shard_map(
        per_device, mesh=mesh, in_specs=in_specs, out_specs=out_specs, check_vma=False
    )
```

profile of v0, /device:TPU:0, one launch (start us, length us, event | category | flops | bytes accessed | tf_op | source)
XLA Modules:
  0.0 1267.5 jit_solution(7760785568148674721)
XLA Ops:
  36.3 54.6 %all-gather.13.cloned.1.call-done = bf16[1152,3,576]{2,0,1:T(8,128)(2,1)} async-done(((bf16[288,3,576]{2,0,1:T(8,128)(2,1)}), bf16[1152,3,576]{2,0,1:T(8,128)(2,1)}) %all-gather.13.cloned.1.call-update) | async-done | bytes 3981328 | tf_op jit(solution)/shard_map/all_gather | solution.py:120
  90.9 10.7 fusion.59
  109.1 57.2 %while.28 = (s32[]{:T(128)}, bf16[2,729,8,72]{1,3,2,0:T(8,128)(2,1)}, f32[2,8,729]{2,1,0:T(8,128)S(1)}, bf16[2,729,8,72]{1,3,2,0:T(8,128)(2,1)}, bf16[2,729,8,72...) while((s32[]{:T(128)}, bf16[2,729,8,72]{1,3,2,0:T(8,128)(2,1)}, ...), condition=%wide.region_5.6_spmd, body=%wide.region_2.5_spmd.sunk | while | flops 1263117824 | bytes 55831608 | solution.py:160
  202.4 102.8 %all-gather.23.cloned.1.call-done = bf16[4,729,1152]{2,1,0:T(8,128)(2,1)} async-done(((bf16[1,729,1152]{2,1,0:T(8,128)(2,1)}), bf16[4,729,1152]{2,1,0:T(8,128)(2,1)}) %all-gather.23.cloned.1.call-update) | async-done | bytes 6718480 | tf_op jit(solution)/shard_map/all_gather | solution.py:222
  310.0 34.9 %all-gather.21.cloned.1.call-done = bf16[1152,1076]{1,0:T(8,128)(2,1)} async-done(((bf16[288,1076]{1,0:T(8,128)(2,1)}), bf16[1152,1076]{1,0:T(8,128)(2,1)}) %all-gather.21.cloned.1.call-update) | async-done | bytes 2479120 | tf_op jit(solution)/shard_map/all_gather | solution.py:123
  344.9 14.5 %fusion.69 = f32[4,729,1076]{1,2,0:T(8,128)} fusion(bf16[4,729,1152]{2,1,0:T(8,128)(2,1)} %all-gather.23.cloned.1.call-done, bf16[1152,1076]{1,0:T(8,128)(2,1)} %all-gather.21.cloned.1.call-done), kind=kOutput, calls=%fused_computation.114 | convolution fusion | flops 7229067264 | bytes 21748032 | tf_op jit(solution)/shard_map/isd,df->isf/dot_general | solution.py:226
  359.9 13.3 %all-gather.1 = bf16[4,729,16]{1,2,0:T(8,128)(2,1)S(1)} all-gather(bf16[1,729,16]{1,2,0:T(8,128)(2,1)S(1)} %fusion.92), channel_id=2, replica_groups=mesh['fsdp'=4,'heads'=2,'tensor'=4] {'tensor'}, dimensions={0}, use_global_device_ids=true | all-gather | bytes 116640 | tf_op jit(solution)/shard_map/all_gather | solution.py:189
  373.2 13.1 %all-gather.19.cloned.1.call-done = bf16[1152,1076]{1,0:T(8,128)(2,1)} async-done(((bf16[288,1076]{1,0:T(8,128)(2,1)}), bf16[1152,1076]{1,0:T(8,128)(2,1)}) %all-gather.19.cloned.1.call-update) | async-done | bytes 2479120 | tf_op jit(solution)/shard_map/all_gather | solution.py:122
  386.4 124.8 %all-gather.17.cloned.1.call-done = bf16[4,729,1152]{2,1,0:T(8,128)(2,1)} async-done(((bf16[1,729,1152]{2,1,0:T(8,128)(2,1)}), bf16[4,729,1152]{2,1,0:T(8,128)(2,1)}) %all-gather.17.cloned.1.call-update) | async-done | bytes 6718480 | tf_op jit(solution)/shard_map/all_gather | solution.py:188
  511.2 12.4 fusion.75
  533.7 18.5 %fusion.50 = bf16[4,729,1076]{1,2,0:T(8,128)(2,1)S(1)} fusion(f32[4,729,1076]{1,2,0:T(8,128)} %get-tuple-element.204, f32[4,729,1076]{1,2,0:T(8,128)} %fusion.69, f32[4,16,729]{2,1,0:T(8,128)S(1)} %fusion.138, bf16[4,16,1076]{2,1,0:T(8,128)(2,1)S(1)} %gather_fusion.7), kind=kOutput, calls=%fused_computation.72 | convolution fusion | flops 668312192 | bytes 31700512 | tf_op jit(solution)/shard_map/cbd,cdp->cbp/dot_general | solution.py:227
  555.9 13.1 %fusion.73 = f32[4,729,1152]{2,1,0:T(8,128)} fusion(bf16[4,729,1076]{1,2,0:T(8,128)(2,1)S(1)} %fusion.50, bf16[1152,1076]{1,0:T(8,128)(2,1)S(1)} %copy-done.56), kind=kOutput, calls=%fused_computation.118 | convolution fusion | flops 7229067264 | bytes 22191264 | tf_op jit(solution)/shard_map/isf,df->isd/dot_general | solution.py:235
  569.0 10.8 add_convert_fusion
  583.9 13.5 %fusion.71 = f32[4,729,1152]{2,1,0:T(8,128)S(1)} fusion(bf16[4,729,1076]{1,2,0:T(8,128)(2,1)} %get-tuple-element.203, bf16[1152,1076]{1,0:T(8,128)(2,1)S(1)} %copy-done.55), kind=kOutput, calls=%fused_computation.116 | convolution fusion | flops 7229067264 | bytes 22191264 | tf_op jit(solution)/shard_map/isf,df->isd/dot_general | solution.py:210
  606.6 90.2 %reduce-scatter.9.cloned.1.call-done = bf16[1,729,1152]{2,1,0:T(8,128)(2,1)} async-done(((bf16[4,729,1152]{2,1,0:T(8,128)(2,1)}), bf16[1,729,1152]{2,1,0:T(8,128)(2,1)}) %reduce-scatter.9.cloned.1.call-update) | async-done | bytes 1679632 | tf_op jit(solution)/shard_map/reduce_scatter | solution.py:242
  700.4 118.0 %reduce-scatter.7.cloned.1.call-done = bf16[1,729,1152]{2,1,0:T(8,128)(2,1)} async-done(((bf16[4,729,1152]{2,1,0:T(8,128)(2,1)}), bf16[1,729,1152]{2,1,0:T(8,128)(2,1)}) %reduce-scatter.7.cloned.1.call-update) | async-done | bytes 1679632 | tf_op jit(solution)/shard_map/reduce_scatter | solution.py:217
  863.4 99.9 %while.29 = (s32[]{:T(128)}, bf16[2,729,8,72]{1,3,2,0:T(8,128)(2,1)}, bf16[2,729,8,72]{1,3,2,0:T(8,128)(2,1)}, bf16[2,729,8,72]{1,3,2,0:T(8,128)(2,1)}, bf16[2,7...) while((s32[]{:T(128)}, ...), condition=%wide.region_15.16_spmd, body=%wide.region_13.15_spmd.sunk | while | flops 3112952320 | bytes 200497152 | solution.py:272
  882.1 12.7 %multiply_reduce_fusion.9 = (f32[8,729]{1,0:T(8,128)S(1)}, f32[8,729,729]{1,2,0:T(8,128)}) fusion(f32[8,729,729]{1,2,0:T(8,128)} %fusion.216, f32[8,729]{1,0:T(8,128)S(1)} %dynamic-slice_bitcast_fusion.2, bf16[2,729,8,72]{1,3,2,0:T(8,128)(2,1)S(1)} %copy-done.13, s32[]{:T(128)S(6)} %copy.187, bf16[2,729,8,72]{1,3,2,0:T(8,128)(2,1)S(1)} %copy-done.9), kind=kOutput, calls=%fused_computation.30.clone.1 | convolution fusion | flops 629220288 | bytes 35830624 | tf_op jit(solution)/shard_map/while/body/eval_jaxpr/qhd,khd->hqk/dot_general | solution.py:58
  894.8 13.2 %multiply_convert_fusion.3 = bf16[8,729,729]{1,2,0:T(8,128)(2,1)S(1)} fusion(f32[8,729,729]{1,2,0:T(8,128)} %get-tuple-element.305, f32[8,729,729]{1,2,0:T(8,128)} %fusion.216, f32[8,729]{1,0:T(8,128)S(1)} %get-tuple-element.306, f32[8,729]{1,0:T(8,128)S(1)} %dynamic-slice_bitcast_fusion.2), kind=kLoop, calls=%fused_computation.29.clone.1 | loop fusion | flops 21257640 | bytes 42561936 | tf_op jit(solution)/shard_map/while/body/eval_jaxpr/convert_element_type | solution.py:63
  932.0 12.6 multiply_reduce_fusion.9
  944.5 13.1 %multiply_convert_fusion.3 = bf16[8,729,729]{1,2,0:T(8,128)(2,1)S(1)} fusion(f32[8,729,729]{1,2,0:T(8,128)} %get-tuple-element.305, f32[8,729,729]{1,2,0:T(8,128)} %fusion.216, f32[8,729]{1,0:T(8,128)S(1)} %get-tuple-element.306, f32[8,729]{1,0:T(8,128)S(1)} %dynamic-slice_bitcast_fusion.2), kind=kLoop, calls=%fused_computation.29.clone.1 | loop fusion | flops 21257640 | bytes 42561936 | tf_op jit(solution)/shard_map/while/body/eval_jaxpr/convert_element_type | solution.py:63
  983.7 11.9 fusion.57
  1011.3 76.5 %all-reduce.9.cloned.1.call-done = (f32[3,8,16,576]{3,1,2,0:T(8,128)}, f32[8,576,16]{1,0,2:T(8,128)}) async-done(((f32[3,8,16,576]{3,1,2,0:T(8,128)}, f32[8,576,16]{1,0,2:T(8,128)}), (f32[3,8,16,576]{3,1,2,0:T(8,128)}, f32[8,576,16]{1,0,2:T(8,128)})) %all-reduce.9.cloned.1.call-update) | async-done | bytes 1179664 | tf_op jit(solution)/shard_map/psum | solution.py:321
  1091.8 142.8 %all-reduce.7.cloned.1.call-done = (f32[3,8,1152,16]{2,1,3,0:T(8,128)}, f32[8,16,1152]{2,0,1:T(8,128)}, f32[8,1152,16]{1,0,2:T(8,128)}, f32[8,16,1152]{2,0,1:T(8,128)}) async-done(((f32[3,8,1152,16]{2,1,3,0:T(8,128)}, f32[8,16,1152]{2,0,1:T(8,128)}, f32[8,1152,16]{1,0,2:T(8,128)}, f32[8,16,1152]{2,0,1:T(8,128)}), (f32[3,8,1152,16]{2,1,3,0:T(8,128)}, f32[8,16,1152]{2,0,1:T(8,128)}, f32[8,1152,16]{1,0,2:T(8,128)}, ...) | async-done | bytes 3538960 | tf_op jit(solution)/shard_map/psum | solution.py:317
  (296 shorter events, 320.1 us)
Async XLA Ops:
  8.0 17.2 %copy-start = (bf16[3,8,1152,16]{2,3,1,0:T(8,128)(2,1)S(1)}, bf16[3,8,1152,16]{2,3,1,0:T(8,128)(2,1)}, u32[]{:S(2)}) copy-start(bf16[3,8,1152,16]{2,3,1,0:T(8,128)(2,1)} %param.38) | copy-start | bytes 2654212
  8.0 25.2 %all-gather.11.cloned.1.call-start = ((), (), s32[]{:S(2)}) async-start(), calls=%async_computation.4 | async-start | bytes 5087232 | tf_op jit(solution)/shard_map/all_gather | solution.py:126
  17.9 73.0 %all-gather.13.cloned.1.call-start = ((), (), s32[]{:S(2)}) async-start(), calls=%async_computation.5 | async-start | bytes 5529600 | tf_op jit(solution)/shard_map/all_gather | solution.py:120
  18.6 150.3 %all-gather.15.cloned.1.call-start = ((), (), s32[]{:S(2)}) async-start(), calls=%async_computation.6 | async-start | bytes 1843200 | tf_op jit(solution)/shard_map/all_gather | solution.py:121
  19.4 170.4 %reduce-scatter.5.cloned.1.call-start = ((), (), s32[]{:S(2)}) async-start(), calls=%async_computation.7 | async-start | bytes 5087232 | tf_op jit(solution)/shard_map/reduce_scatter | solution.py:176
  25.2 76.4 %copy-start.32 = (bf16[2,3,16,576]{3,2,1,0:T(8,128)(2,1)}, bf16[2,3,16,576]{3,2,1,0:T(8,128)(2,1)S(1)}, u32[]{:S(2)}) copy-start(bf16[2,3,16,576]{3,2,1,0:T(8,128)(2,1)S(1)} %gather_fusion.2) | copy-start | bytes 331780
  25.8 75.8 %copy-start.11 = (bf16[2,3,1152,16]{2,3,1,0:T(8,128)(2,1)}, bf16[2,3,1152,16]{2,3,1,0:T(8,128)(2,1)S(1)}, u32[]{:S(2)}) copy-start(bf16[2,3,1152,16]{2,3,1,0:T(8,128)(2,1)S(1)} %gather_fusion.1) | copy-start | bytes 663556
  36.3 65.4 %copy-start.25 = (f32[3,2,729,16]{2,3,0,1:T(8,128)}, f32[3,2,729,16]{2,3,0,1:T(8,128)S(1)}, u32[]{:S(2)}) copy-start(f32[3,2,729,16]{2,3,0,1:T(8,128)S(1)} %fusion.86) | copy-start | bytes 839812
  109.1 57.2 %copy-start.21 = (bf16[2,576,16]{1,2,0:T(8,128)(2,1)S(1)}, bf16[2,576,16]{1,2,0:T(8,128)(2,1)}, u32[]{:S(2)}) copy-start(bf16[2,576,16]{1,2,0:T(8,128)(2,1)} %gather_fusion.3) | copy-start | bytes 110596
  178.4 126.8 %all-gather.23.cloned.1.call-start = ((), (), s32[]{:S(2)}) async-start(), calls=%async_computation.12 | async-start | bytes 8478720 | tf_op jit(solution)/shard_map/all_gather | solution.py:222
  181.8 163.1 %all-gather.21.cloned.1.call-start = ((), (), s32[]{:S(2)}) async-start(), calls=%async_computation.10 | async-start | bytes 3317760 | tf_op jit(solution)/shard_map/all_gather | solution.py:123
  182.4 204.0 %all-gather.19.cloned.1.call-start = ((), (), s32[]{:S(2)}) async-start(), calls=%async_computation.9 | async-start | bytes 3317760 | tf_op jit(solution)/shard_map/all_gather | solution.py:122
  182.9 328.3 %all-gather.17.cloned.1.call-start = ((), (), s32[]{:S(2)}) async-start(), calls=%async_computation.8 | async-start | bytes 8478720 | tf_op jit(solution)/shard_map/all_gather | solution.py:188
  196.7 500.0 %reduce-scatter.9.cloned.1.call-start = ((), (), s32[]{:S(2)}) async-start(), calls=%async_computation.13 | async-start | bytes 8478720 | tf_op jit(solution)/shard_map/reduce_scatter | solution.py:242
  310.0 49.4 %copy-start.14 = (bf16[1,729,1152]{2,1,0:T(8,128)(2,1)S(1)}, bf16[1,729,1152]{2,1,0:T(8,128)(2,1)}, u32[]{:S(2)}) copy-start(bf16[1,729,1152]{2,1,0:T(8,128)(2,1)} %add_convert_fusion.4) | copy-start | bytes 5038852
  373.2 150.3 %copy-start.34 = (bf16[4,729,16]{1,2,0:T(8,128)(2,1)}, bf16[4,729,16]{1,2,0:T(8,128)(2,1)S(1)}, u32[]{:S(2)}) copy-start(bf16[4,729,16]{1,2,0:T(8,128)(2,1)S(1)} %all-gather.1) | copy-start | bytes 279940
  579.8 238.6 %reduce-scatter.7.cloned.1.call-start = ((), (), s32[]{:S(2)}) async-start(), calls=%async_computation.11 | async-start | bytes 8478720 | tf_op jit(solution)/shard_map/reduce_scatter | solution.py:217
  605.9 245.4 %all-gather.25.cloned.1.call-start = ((), (), s32[]{:S(2)}) async-start(), calls=%async_computation.14 | async-start | bytes 5087232 | tf_op jit(solution)/shard_map/all_gather | solution.py:261
  696.8 121.6 %copy-start.18 = (bf16[1,729,1152]{2,1,0:T(8,128)(2,1)S(1)}, bf16[1,729,1152]{2,1,0:T(8,128)(2,1)}, u32[]{:S(2)}) copy-start(bf16[1,729,1152]{2,1,0:T(8,128)(2,1)} %reduce-scatter.9.cloned.1.call-done) | copy-start | bytes 5038852
  824.8 175.7 %all-reduce.11.cloned.1.call-start = ((), (), s32[]{:S(2)}) async-start(), calls=%async_computation.18 | async-start | bytes 1179648 | tf_op jit(solution)/shard_map/psum | solution.py:325
  851.2 236.6 %all-reduce.9.cloned.1.call-start = ((), (), s32[]{:S(2)}) async-start(), calls=%async_computation.17 | async-start | bytes 2621440 | tf_op jit(solution)/shard_map/psum | solution.py:321
  863.4 99.9 %copy-start.26 = (f32[3,2,729,16]{2,3,0,1:T(8,128)S(1)}, f32[3,2,729,16]{2,3,0,1:T(8,128)}, u32[]{:S(2)}) copy-start(f32[3,2,729,16]{2,3,0,1:T(8,128)} %copy-done.25) | copy-start | bytes 839812
  972.4 262.2 %all-reduce.7.cloned.1.call-start = ((), (), s32[]{:S(2)}) async-start(), calls=%async_computation.16 | async-start | bytes 7077888 | tf_op jit(solution)/shard_map/psum | solution.py:317
  983.7 263.7 %reduce-scatter.11.cloned.1.call-start = ((), (), s32[]{:S(2)}) async-start(), calls=%async_computation.15 | async-start | bytes 5087232 | tf_op jit(solution)/shard_map/reduce_scatter | solution.py:292
  (68 other events, 420.4 us)
Sparse Core Ops, SparseCore 0:
  18.0 15.1 all-gather.10
  35.0 55.7 all-gather.12
  92.7 30.1 all-gather.14
  178.5 11.2 reduce-scatter.4
  824.9 12.9 all-gather.24
  851.3 55.7 all-reduce.10
  972.6 115.1 all-reduce.8
  1094.9 139.7 all-reduce.6
  1237.0 10.2 reduce-scatter.10
Sparse Core Ops, SparseCore 1:
  181.9 123.2 all-gather.22
  306.9 37.9 all-gather.20
  346.6 39.7 all-gather.18
  387.9 123.2 all-gather.16
  579.9 116.8 reduce-scatter.8
  699.2 119.1 reduce-scatter.6
where the time goes:
time: 1270 us
  waiting for transfers between devices  781 us (61%)
  matrix products  326 us (26%)
  other arithmetic  77 us (6%)
  local copies, waits for them, and re-layouts  49.9 us (4%)
  between operations  18.4 us (1%)
  blocking collectives  13.3 us (1%)
    psum x1, waiting for transfers between devices, per_device(): lax.psum((grad_qkv_in_part, grad_proj_out_part, grad_up_in_part, grad_dow...  143 us
    all_gather x1, waiting for transfers between devices, per_device(): lax.all_gather(second_norm_reduced, 'tensor', axis=0, tiled=True)  125 us
    reduce_scatter x1, waiting for transfers between devices, per_device(): lax.psum_scatter(mlp_part.astype(jnp.bfloat16), 'tensor', scatter_dimensi...  118 us
    all_gather x1, waiting for transfers between devices, per_device(): grad_mlp_in = lax.all_gather(grad_mlp, 'tensor', axis=0, tiled=True)  103 us
    reduce_scatter x1, waiting for transfers between devices, per_device(): lax.psum_scatter(grad_ln2.astype(jnp.bfloat16), 'tensor', scatter_dimensi...  90.2 us
    psum x1, waiting for transfers between devices, per_device(): lax.psum((grad_qkv_out_part, grad_proj_in_part), ('fsdp', 'tensor'))  76.5 us
    all_gather x1, waiting for transfers between devices, per_device(): lax.all_gather(query_key_value_weight, 'fsdp', axis=0, tiled=True)  54.6 us
    unnamed x129, local copies, waits for them, and re-layouts  35.5 us
  transfers between devices with their start and end apart: 15, of which 12 were waited for; matrix products, arithmetic and copies ran while one was open for 27% of the time, Pallas kernels for 0%

commit v1 on v0

--- a/solution.py
+++ b/solution.py
@@ -315,8 +315,11 @@
         ),
     )
     grad_qkv_in, grad_proj_out, grad_up_in, grad_down_out = lax.psum(
-        (grad_qkv_in_part, grad_proj_out_part, grad_up_in_part, grad_down_out_part),
-        ("fsdp", "heads", "tensor"),
+        lax.psum(
+            (grad_qkv_in_part, grad_proj_out_part, grad_up_in_part, grad_down_out_part),
+            ("heads", "tensor"),
+        ),
+        "fsdp",
     )
     grad_qkv_out, grad_proj_in = lax.psum(
         (grad_qkv_out_part, grad_proj_in_part), ("fsdp", "tensor")

time: 1270 us -> 1360 us (1.071)
  waiting for transfers between devices: 781 us -> 866 us
    psum x0 -> x1, waiting for transfers between devices: none -> 93.4 us  [per_device(): lax.psum(lax.psum((grad_qkv_in_part, grad_proj_out_part, grad_up_in_part,...]
    psum x1, waiting for transfers between devices: 143 us -> 60.8 us  [per_device(): lax.psum((grad_qkv_in_part, grad_proj_out_part, grad_up_in_part, grad_dow...]
    psum x1, waiting for transfers between devices: 0.02 us -> 42.1 us  [per_device(): lax.psum(grad_up_out_part.astype(jnp.bfloat16), ('fsdp', 'heads'))]
    psum x1, waiting for transfers between devices: 76.5 us -> 109 us  [per_device(): lax.psum((grad_qkv_out_part, grad_proj_in_part), ('fsdp', 'tensor'))]
    unnamed x129 -> x121, local copies, waits for them, and re-layouts: 35.5 us -> 34.7 us
  transfers between devices with their start and end apart: 15 -> 16, of which waited for: 12 -> 14; matrix products, arithmetic and copies ran while one was open for 27% -> 17% of each run, Pallas kernels for 0% -> 0%
where the time goes in v1:
time: 1360 us
  waiting for transfers between devices  866 us (64%)
  matrix products  329 us (24%)
  other arithmetic  77.4 us (6%)
  local copies, waits for them, and re-layouts  49.9 us (4%)
  between operations  18.7 us (1%)
    all_gather x1, waiting for transfers between devices, per_device(): lax.all_gather(second_norm_reduced, 'tensor', axis=0, tiled=True)  125 us
    reduce_scatter x1, waiting for transfers between devices, per_device(): lax.psum_scatter(mlp_part.astype(jnp.bfloat16), 'tensor', scatter_dimensi...  118 us
    psum x1, waiting for transfers between devices, per_device(): lax.psum((grad_qkv_out_part, grad_proj_in_part), ('fsdp', 'tensor'))  109 us
    all_gather x1, waiting for transfers between devices, per_device(): grad_mlp_in = lax.all_gather(grad_mlp, 'tensor', axis=0, tiled=True)  102 us
    psum x1, waiting for transfers between devices, per_device(): lax.psum(lax.psum((grad_qkv_in_part, grad_proj_out_part, grad_up_in_part,...  93.4 us
    reduce_scatter x1, waiting for transfers between devices, per_device(): lax.psum_scatter(grad_ln2.astype(jnp.bfloat16), 'tensor', scatter_dimensi...  90.3 us
    psum x1, waiting for transfers between devices, per_device(): lax.psum((grad_qkv_in_part, grad_proj_out_part, grad_up_in_part, grad_dow...  60.8 us
    all_gather x1, waiting for transfers between devices, per_device(): lax.all_gather(query_key_value_weight, 'fsdp', axis=0, tiled=True)  54.6 us
  transfers between devices with their start and end apart: 16, of which 14 were waited for; matrix products, arithmetic and copies ran while one was open for 17% of the time, Pallas kernels for 0%

profile of v1, /device:TPU:0, one launch (start us, length us, event | category | flops | bytes accessed | tf_op | source)
XLA Modules:
  0.0 1356.4 jit_solution(8893954172976958505)
XLA Ops:
  36.3 54.6 %all-gather.13.cloned.1.call-done = bf16[1152,3,576]{2,0,1:T(8,128)(2,1)} async-done(((bf16[288,3,576]{2,0,1:T(8,128)(2,1)}), bf16[1152,3,576]{2,0,1:T(8,128)(2,1)}) %all-gather.13.cloned.1.call-update) | async-done | bytes 3981328 | tf_op jit(solution)/shard_map/all_gather | solution.py:120
  109.1 57.1 %while.28 = (s32[]{:T(128)}, bf16[2,729,8,72]{1,3,2,0:T(8,128)(2,1)}, f32[2,8,729]{2,1,0:T(8,128)S(1)}, bf16[2,729,8,72]{1,3,2,0:T(8,128)(2,1)}, bf16[2,729,8,72...) while((s32[]{:T(128)}, bf16[2,729,8,72]{1,3,2,0:T(8,128)(2,1)}, ...), condition=%wide.region_5.6_spmd, body=%wide.region_2.5_spmd.sunk | while | flops 1263117824 | bytes 55831608 | solution.py:160
  202.6 101.7 %all-gather.23.cloned.1.call-done = bf16[4,729,1152]{2,1,0:T(8,128)(2,1)} async-done(((bf16[1,729,1152]{2,1,0:T(8,128)(2,1)}), bf16[4,729,1152]{2,1,0:T(8,128)(2,1)}) %all-gather.23.cloned.1.call-update) | async-done | bytes 6718480 | tf_op jit(solution)/shard_map/all_gather | solution.py:222
  309.2 34.9 %all-gather.21.cloned.1.call-done = bf16[1152,1076]{1,0:T(8,128)(2,1)} async-done(((bf16[288,1076]{1,0:T(8,128)(2,1)}), bf16[1152,1076]{1,0:T(8,128)(2,1)}) %all-gather.21.cloned.1.call-update) | async-done | bytes 2479120 | tf_op jit(solution)/shard_map/all_gather | solution.py:123
  344.0 14.7 %fusion.69 = f32[4,729,1076]{1,2,0:T(8,128)} fusion(bf16[4,729,1152]{2,1,0:T(8,128)(2,1)} %all-gather.23.cloned.1.call-done, bf16[1152,1076]{1,0:T(8,128)(2,1)} %all-gather.21.cloned.1.call-done), kind=kOutput, calls=%fused_computation.114 | convolution fusion | flops 7229067264 | bytes 21748032 | tf_op jit(solution)/shard_map/isd,df->isf/dot_general | solution.py:226
  359.3 13.4 all-gather.1
  372.7 12.8 all-gather.19.cloned.1.call-done
  385.5 124.8 %all-gather.17.cloned.1.call-done = bf16[4,729,1152]{2,1,0:T(8,128)(2,1)} async-done(((bf16[1,729,1152]{2,1,0:T(8,128)(2,1)}), bf16[4,729,1152]{2,1,0:T(8,128)(2,1)}) %all-gather.17.cloned.1.call-update) | async-done | bytes 6718480 | tf_op jit(solution)/shard_map/all_gather | solution.py:188
  510.4 12.6 fusion.75
  533.1 18.4 %fusion.50 = bf16[4,729,1076]{1,2,0:T(8,128)(2,1)S(1)} fusion(f32[4,729,1076]{1,2,0:T(8,128)} %get-tuple-element.208, f32[4,729,1076]{1,2,0:T(8,128)} %fusion.69, f32[4,16,729]{2,1,0:T(8,128)S(1)} %fusion.138, bf16[4,16,1076]{2,1,0:T(8,128)(2,1)S(1)} %gather_fusion.7), kind=kOutput, calls=%fused_computation.72 | convolution fusion | flops 668312192 | bytes 31700512 | tf_op jit(solution)/shard_map/cbd,cdp->cbp/dot_general | solution.py:227
  555.3 13.3 fusion.73
  583.4 13.4 fusion.71
  606.0 90.3 %reduce-scatter.9.cloned.1.call-done = bf16[1,729,1152]{2,1,0:T(8,128)(2,1)} async-done(((bf16[4,729,1152]{2,1,0:T(8,128)(2,1)}), bf16[1,729,1152]{2,1,0:T(8,128)(2,1)}) %reduce-scatter.9.cloned.1.call-update) | async-done | bytes 1679632 | tf_op jit(solution)/shard_map/reduce_scatter | solution.py:242
  699.8 118.1 %reduce-scatter.7.cloned.1.call-done = bf16[1,729,1152]{2,1,0:T(8,128)(2,1)} async-done(((bf16[4,729,1152]{2,1,0:T(8,128)(2,1)}), bf16[1,729,1152]{2,1,0:T(8,128)(2,1)}) %reduce-scatter.7.cloned.1.call-update) | async-done | bytes 1679632 | tf_op jit(solution)/shard_map/reduce_scatter | solution.py:217
  848.2 99.5 %while.29 = (s32[]{:T(128)}, bf16[2,729,8,72]{1,3,2,0:T(8,128)(2,1)}, bf16[2,729,8,72]{1,3,2,0:T(8,128)(2,1)}, bf16[2,729,8,72]{1,3,2,0:T(8,128)(2,1)}, bf16[2,7...) while((s32[]{:T(128)}, ...), condition=%wide.region_15.16_spmd, body=%wide.region_13.15_spmd.sunk | while | flops 3112952320 | bytes 200497152 | solution.py:272
  866.6 12.5 multiply_reduce_fusion.9
  879.1 13.2 multiply_convert_fusion.3
  916.3 12.5 multiply_reduce_fusion.9
  928.8 13.2 multiply_convert_fusion.3
  985.4 60.8 %all-reduce.11.cloned.1.call-done = (f32[3,8,1152,16]{2,1,3,0:T(8,128)}, f32[8,16,1152]{2,0,1:T(8,128)}, f32[8,1152,16]{1,0,2:T(8,128)}, f32[8,16,1152]{2,0,1:T(8,128)}) async-done(((f32[3,8,1152,16]{2,1,3,0:T(8,128)}, f32[8,16,1152]{2,0,1:T(8,128)}, f32[8,1152,16]{1,0,2:T(8,128)}, f32[8,16,1152]{2,0,1:T(8,128)}), (f32[3,8,1152,16]{2,1,3,0:T(8,128)}, f32[8,16,1152]{2,0,1:T(8,128)}, ...) | async-done | bytes 3538960 | tf_op jit(solution)/shard_map/psum | solution.py:318
  1046.7 11.8 fusion.57
  1063.3 42.1 %all-reduce.15.cloned.1.call-done = (bf16[8,16,1076]{2,0,1:T(8,128)(2,1)}, bf16[8,16,1076]{2,0,1:T(8,128)(2,1)}) async-done(((bf16[8,16,1076]{2,0,1:T(8,128)(2,1)}, bf16[8,16,1076]{2,0,1:T(8,128)(2,1)}), (bf16[8,16,1076]{2,0,1:T(8,128)(2,1)}, bf16[8,16,1076]{2,0,1:T(8,128)(2,1)})) %all-reduce.15.cloned.1.call-update) | async-done | bytes 550928 | tf_op jit(solution)/shard_map/psum | solution.py:328
  1116.2 108.9 %all-reduce.9.cloned.1.call-done = (f32[3,8,16,576]{3,1,2,0:T(8,128)}, f32[8,576,16]{1,0,2:T(8,128)}) async-done(((f32[3,8,16,576]{3,1,2,0:T(8,128)}, f32[8,576,16]{1,0,2:T(8,128)}), (f32[3,8,16,576]{3,1,2,0:T(8,128)}, f32[8,576,16]{1,0,2:T(8,128)})) %all-reduce.9.cloned.1.call-update) | async-done | bytes 1179664 | tf_op jit(solution)/shard_map/psum | solution.py:324
  1229.2 93.4 %all-reduce.13.cloned.1.call-done = (f32[3,8,1152,16]{2,1,3,0:T(8,128)}, f32[8,16,1152]{2,0,1:T(8,128)}, f32[8,1152,16]{1,0,2:T(8,128)}, f32[8,16,1152]{2,0,1:T(8,128)}) async-done(((f32[3,8,1152,16]{2,1,3,0:T(8,128)}, f32[8,16,1152]{2,0,1:T(8,128)}, f32[8,1152,16]{1,0,2:T(8,128)}, f32[8,16,1152]{2,0,1:T(8,128)}), (f32[3,8,1152,16]{2,1,3,0:T(8,128)}, f32[8,16,1152]{2,0,1:T(8,128)}, ...) | async-done | bytes 3538960 | tf_op jit(solution)/shard_map/psum | solution.py:317
  (290 shorter events, 345.8 us)
Async XLA Ops:
  8.0 25.2 %all-gather.11.cloned.1.call-start = ((), (), s32[]{:S(2)}) async-start(), calls=%async_computation.4 | async-start | bytes 5087232 | tf_op jit(solution)/shard_map/all_gather | solution.py:126
  17.9 73.0 %all-gather.13.cloned.1.call-start = ((), (), s32[]{:S(2)}) async-start(), calls=%async_computation.5 | async-start | bytes 5529600 | tf_op jit(solution)/shard_map/all_gather | solution.py:120
  18.6 149.4 %all-gather.15.cloned.1.call-start = ((), (), s32[]{:S(2)}) async-start(), calls=%async_computation.6 | async-start | bytes 1843200 | tf_op jit(solution)/shard_map/all_gather | solution.py:121
  19.4 169.6 %reduce-scatter.5.cloned.1.call-start = ((), (), s32[]{:S(2)}) async-start(), calls=%async_computation.7 | async-start | bytes 5087232 | tf_op jit(solution)/shard_map/reduce_scatter | solution.py:176
  25.6 76.0 %copy-start.32 = (bf16[2,3,16,576]{3,2,1,0:T(8,128)(2,1)}, bf16[2,3,16,576]{3,2,1,0:T(8,128)(2,1)S(1)}, u32[]{:S(2)}) copy-start(bf16[2,3,16,576]{3,2,1,0:T(8,128)(2,1)S(1)} %gather_fusion.2) | copy-start | bytes 331780
  26.2 75.4 %copy-start.9 = (bf16[2,3,1152,16]{2,3,1,0:T(8,128)(2,1)}, bf16[2,3,1152,16]{2,3,1,0:T(8,128)(2,1)S(1)}, u32[]{:S(2)}) copy-start(bf16[2,3,1152,16]{2,3,1,0:T(8,128)(2,1)S(1)} %gather_fusion.1) | copy-start | bytes 663556
  36.3 65.4 %copy-start.21 = (f32[3,2,729,16]{2,3,0,1:T(8,128)}, f32[3,2,729,16]{2,3,0,1:T(8,128)S(1)}, u32[]{:S(2)}) copy-start(f32[3,2,729,16]{2,3,0,1:T(8,128)S(1)} %fusion.86) | copy-start | bytes 839812
  177.5 126.8 %all-gather.23.cloned.1.call-start = ((), (), s32[]{:S(2)}) async-start(), calls=%async_computation.12 | async-start | bytes 8478720 | tf_op jit(solution)/shard_map/all_gather | solution.py:222
  181.0 163.1 %all-gather.21.cloned.1.call-start = ((), (), s32[]{:S(2)}) async-start(), calls=%async_computation.10 | async-start | bytes 3317760 | tf_op jit(solution)/shard_map/all_gather | solution.py:123
  181.6 203.9 %all-gather.19.cloned.1.call-start = ((), (), s32[]{:S(2)}) async-start(), calls=%async_computation.9 | async-start | bytes 3317760 | tf_op jit(solution)/shard_map/all_gather | solution.py:122
  182.1 328.2 %all-gather.17.cloned.1.call-start = ((), (), s32[]{:S(2)}) async-start(), calls=%async_computation.8 | async-start | bytes 8478720 | tf_op jit(solution)/shard_map/all_gather | solution.py:188
  196.0 500.3 %reduce-scatter.9.cloned.1.call-start = ((), (), s32[]{:S(2)}) async-start(), calls=%async_computation.13 | async-start | bytes 8478720 | tf_op jit(solution)/shard_map/reduce_scatter | solution.py:242
  198.6 638.3 %copy-start.47 = (s32[4]{0:T(128)}, s32[4]{0:T(128)S(1)}, u32[]{:S(2)}) copy-start(s32[4]{0:T(128)S(1)} %gather_fusion.5) | copy-start | bytes 52
  309.2 223.9 %copy-start.25 = (f32[4,16,729]{2,1,0:T(8,128)}, f32[4,16,729]{2,1,0:T(8,128)S(1)}, u32[]{:S(2)}) copy-start(f32[4,16,729]{2,1,0:T(8,128)S(1)} %fusion.138) | copy-start | bytes 559876
  372.7 150.3 %copy-start.34 = (bf16[4,729,16]{1,2,0:T(8,128)(2,1)}, bf16[4,729,16]{1,2,0:T(8,128)(2,1)S(1)}, u32[]{:S(2)}) copy-start(bf16[4,729,16]{1,2,0:T(8,128)(2,1)S(1)} %all-gather.1) | copy-start | bytes 279940
  579.3 238.6 %reduce-scatter.7.cloned.1.call-start = ((), (), s32[]{:S(2)}) async-start(), calls=%async_computation.11 | async-start | bytes 8478720 | tf_op jit(solution)/shard_map/reduce_scatter | solution.py:217
  605.3 232.9 %all-gather.25.cloned.1.call-start = ((), (), s32[]{:S(2)}) async-start(), calls=%async_computation.14 | async-start | bytes 5087232 | tf_op jit(solution)/shard_map/all_gather | solution.py:261
  824.7 221.6 %all-reduce.11.cloned.1.call-start = ((), (), s32[]{:S(2)}) async-start(), calls=%async_computation.17 | async-start | bytes 7077888 | tf_op jit(solution)/shard_map/psum | solution.py:318
  848.2 99.5 %copy-start.20 = (f32[2,729,16]{1,2,0:T(8,128)S(1)}, f32[2,729,16]{1,2,0:T(8,128)}, u32[]{:S(2)}) copy-start(f32[2,729,16]{1,2,0:T(8,128)} %copy-done.19) | copy-start | bytes 279940
  960.1 145.3 %all-reduce.15.cloned.1.call-start = ((), (), s32[]{:S(2)}) async-start(), calls=%async_computation.19 | async-start | bytes 1179648 | tf_op jit(solution)/shard_map/psum | solution.py:328
  975.0 250.2 %all-reduce.9.cloned.1.call-start = ((), (), s32[]{:S(2)}) async-start(), calls=%async_computation.16 | async-start | bytes 2621440 | tf_op jit(solution)/shard_map/psum | solution.py:324
  982.6 64.1 %copy-start.58 = (bf16[2,729,8,72]{1,3,2,0:T(8,128)(2,1)S(1)}, bf16[2,729,8,72]{1,3,2,0:T(8,128)(2,1)}, u32[]{:S(2)}) copy-start(bf16[2,729,8,72]{1,3,2,0:T(8,128)(2,1)} %get-tuple-element.96) | copy-start | bytes 5038852
  985.4 337.2 %all-reduce.13.cloned.1.call-start = ((), (), s32[]{:S(2)}) async-start(), calls=%async_computation.18 | async-start | bytes 7077888 | tf_op jit(solution)/shard_map/psum | solution.py:317
  1046.3 289.8 %reduce-scatter.11.cloned.1.call-start = ((), (), s32[]{:S(2)}) async-start(), calls=%async_computation.15 | async-start | bytes 5087232 | tf_op jit(solution)/shard_map/reduce_scatter | solution.py:292
  (65 other events, 465.6 us)
Sparse Core Ops, SparseCore 0:
  18.0 15.1 all-gather.10
  35.0 55.7 all-gather.12
  92.7 30.1 all-gather.14
  177.7 11.1 reduce-scatter.4
  824.8 13.0 all-gather.24
  960.2 85.9 all-reduce.10
  1050.3 55.0 all-reduce.14
  1111.4 113.6 all-reduce.8
  1229.0 93.5 all-reduce.12
  1324.8 11.1 reduce-scatter.10
Sparse Core Ops, SparseCore 1:
  181.1 123.2 all-gather.22
  306.0 37.9 all-gather.20
  345.7 39.7 all-gather.18
  387.1 123.2 all-gather.16
  579.4 116.8 reduce-scatter.8
  698.8 119.1 reduce-scatter.6
